TPU v7x, 512 devices: a whole 4x8x8 slice. The times are simulated.
512 devices in a mesh: gx: 8 (over y), gy: 4 (over x), gz: 16 (over z, core).
Axes of the slice: x: 4, y: 8, z: 8, core: 2. Of those that a mesh axis runs over, the one named last changes fastest.
Arguments:
- fields: float32 [4, 512, 256, 512], P(None, 'gz', 'gx', 'gy'), may hold values from -6 to 6
- material: int32 [512, 256, 512], P('gz', 'gx', 'gy'), may hold values from 0 to 15
- depth_order: int32 [16], replicated, may hold values from 0 to 15, each once
- table: float32 [4, 16], replicated, may hold values from 0.2 to 2
Outputs:
- image: float32 [4, 256, 512], P(None, ('gx', 'gz'), 'gy')
Inputs may be any that keep to these rules, and one draw needn't show every extreme that they name: `depth_order`: a permutation: each brick layer along gz gets a distinct rank, 0 nearest the viewer.
All inputs are finite; a program needn't handle non-finite values.
Results may differ from a plain program's by a relative error of at most 0.0003.
Values sent between devices are 32-bit elements; how exact they have to be, the bound alone decides.
A program may use at most 64 MiB of HBM per device.

v0:
```python
import jax
import jax.numpy as jnp
from jax import lax
from jax.sharding import PartitionSpec as P

ambient = 0.3
diffuse = 1.2
grad_floor = 0.0025
light_z = 2.0 / 3.0
light_x = 1.0 / 3.0
light_y = 2.0 / 3.0


def extended(cells, sides, width):
    for axis, dim in sides:
        count = lax.axis_size(axis)
        ends = count - 1
        head = lax.slice_in_dim(cells, 0, width, axis=dim)
        tail = lax.slice_in_dim(cells, cells.shape[dim] - width, cells.shape[dim], axis=dim)
        cells = jnp.concatenate(
            [
                lax.ppermute(tail, axis, [(i, (i + 1) % count) for i in range(ends)]),
                cells,
                lax.ppermute(head, axis, [((i + 1) % count, i) for i in range(ends)]),
            ],
            axis=dim,
        )
    return cells


def blur_axis(values, which):
    length = values.shape[which]
    lower = lax.slice_in_dim(values, 0, length - 2, axis=which)
    middle = lax.slice_in_dim(values, 1, length - 1, axis=which)
    upper = lax.slice_in_dim(values, 2, length, axis=which)
    return (lower + 2.0 * middle + upper) * 0.25


def slope_axis(values, which):
    length = values.shape[which]
    lower = lax.slice_in_dim(values, 0, length - 2, axis=which)
    upper = lax.slice_in_dim(values, 2, length, axis=which)
    return (upper - lower) * 0.5


def smooth_all(values):
    for which in (1, 2, 3):
        values = blur_axis(values, which)
    return values


def shade_brick(smoothed, density, material, table, depth_total):
    grad_z = blur_axis(blur_axis(slope_axis(density, 0), 1), 2)
    grad_x = blur_axis(blur_axis(slope_axis(density, 1), 0), 2)
    grad_y = blur_axis(blur_axis(slope_axis(density, 2), 0), 1)
    facing = jnp.abs(light_z * grad_z + light_x * grad_x + light_y * grad_y)
    length = jnp.sqrt(grad_z * grad_z + grad_x * grad_x + grad_y * grad_y + grad_floor)
    shading = ambient + diffuse * facing / length
    entries = table.shape[1]
    onehot = (material[None] == jnp.arange(entries, dtype=jnp.int32)[:, None, None, None]).astype(
        jnp.float32
    )
    looked = jnp.einsum("cm,mzxy->czxy", table, onehot, precision=lax.Precision.HIGHEST)
    extinct = looked[3] * jax.nn.softplus(3.0 * smoothed[0]) * (2.0 / depth_total)
    colour = looked[:3] * shading[None] * (0.5 + jax.nn.sigmoid(2.0 * smoothed[1:]))
    ahead = jnp.cumsum(extinct, axis=0) - extinct
    weight = jnp.exp(-ahead) * -jnp.expm1(-extinct)
    return (jnp.sum(weight[None] * colour, axis=1), jnp.sum(extinct, axis=0))


def on_device(fields, material, depth_order, table):
    zsize = fields.shape[1]
    xsize = fields.shape[2]
    ysize = fields.shape[3]
    layers = lax.axis_size("gz")
    depth_total = zsize * layers
    width_total = xsize * lax.axis_size("gx")
    height_total = ysize * lax.axis_size("gy")
    padded = extended(fields, (("gx", 2), ("gy", 3), ("gz", 1)), 2)
    smoothed = smooth_all(padded)
    zpos = lax.axis_index("gz") * zsize - 1 + jnp.arange(zsize + 2, dtype=jnp.int32)
    xpos = lax.axis_index("gx") * xsize - 1 + jnp.arange(xsize + 2, dtype=jnp.int32)
    ypos = lax.axis_index("gy") * ysize - 1 + jnp.arange(ysize + 2, dtype=jnp.int32)
    inside = (
        ((zpos >= 0) & (zpos < depth_total))[:, None, None]
        & ((xpos >= 0) & (xpos < width_total))[None, :, None]
        & ((ypos >= 0) & (ypos < height_total))[None, None, :]
    )
    density = jnp.where(inside, smoothed[0], jnp.zeros_like(smoothed[0]))
    inner = smoothed[:, 1:-1, 1:-1, 1:-1]
    colour, depth = shade_brick(inner, density, material, table, depth_total)
    rows = xsize // layers
    layer_index = lax.axis_index("gz")
    depths = lax.all_gather(depth[None], "gz", axis=0, tiled=True)
    own_rank = depth_order[layer_index]
    nearer = (depth_order < own_rank).astype(jnp.float32)
    atten = jnp.einsum("g,gxy->xy", nearer, depths, precision=lax.Precision.HIGHEST)
    blended = lax.psum_scatter(
        colour * jnp.exp(-atten)[None], "gz", scatter_dimension=1, tiled=True
    )
    total = lax.dynamic_slice_in_dim(jnp.sum(depths, axis=0), layer_index * rows, rows, 0)
    return jnp.concatenate([blended, (-jnp.expm1(-total))[None]], axis=0)


def solution(mesh):
    return jax.shard_map(
        on_device,
        mesh=mesh,
        in_specs=(P(None, "gz", "gx", "gy"), P("gz", "gx", "gy"), P(), P()),
        out_specs=P(None, ("gx", "gz"), "gy"),
        check_vma=False,
    )
```

profile of v0, /device:TPU:26, one launch (start us, length us, event | category | flops | bytes accessed | tf_op | source)
XLA Modules:
  0.0 145.3 jit_solution(10533029868132336585)
XLA Ops:
  0.0 0.0 copy-start
  0.0 1.3 fusion.63
  1.3 4.7 %collective-permute-start = (f32[4,32,2,128]{3,2,1,0:T(2,128)S(1)}, f32[4,32,2,128]{3,2,1,0:T(2,128)S(1)}, u32[]{:S(2)}, u32[]{:S(2)}) collective-permute-start(f32[4,32,2,128]{3,2,1,0:T(2,128)S(1)} %get-tuple-element.9), channel_id=1, source_target_pairs={{0,64},{64,128},{128,192},{192,256},{256,320},{320,384},{384,448},... | collective-permute-start | bytes 393224 | tf_op jit(solution)/shard_map/ppermute | solution.py:22
  6.0 1.9 %collective-permute-start.1 = (f32[4,32,2,128]{3,2,1,0:T(2,128)S(1)}, f32[4,32,2,128]{3,2,1,0:T(2,128)S(1)}, u32[]{:S(2)}, u32[]{:S(2)}) collective-permute-start(f32[4,32,2,128]{3,2,1,0:T(2,128)S(1)} %get-tuple-element.10), channel_id=1, source_target_pairs={{64,0},{128,64},{192,128},{256,192},{320,256},{384,320},{448,384},... | collective-permute-start | bytes 393224 | tf_op jit(solution)/shard_map/ppermute | solution.py:24
  8.0 0.0 copy-done
  8.0 4.5 %fusion = f32[32,32,128,4]{2,3,1,0:T(4,128)} fusion(s32[32,32,128]{2,1,0:T(8,128)} %param.5, f32[4,16]{1,0:T(4,128)S(1)} %copy-done), kind=kOutput, calls=%fused_computation.1 | convolution fusion | flops 102760448 | bytes 2621696 | tf_op jit(solution)/shard_map/cm,mzxy->czxy/dot_general | solution.py:63
  12.5 0.0 collective-permute-done
  12.5 1.6 %collective-permute-done.1 = f32[4,32,2,128]{3,2,1,0:T(2,128)S(1)} collective-permute-done((f32[4,32,2,128]{3,2,1,0:T(2,128)S(1)}, f32[4,32,2,128]{3,2,1,0:T(2,128)S(1)}, u32[]{:S(2)}, u32[]{:S(2)}) %collective-permute-start.1) | collective-permute-done | bytes 131104 | tf_op jit(solution)/shard_map/ppermute | solution.py:24
  14.1 1.9 %pad_maximum_fusion.6 = f32[4,32,36,128]{3,2,1,0:T(8,128)S(1)} fusion(f32[4,32,2,128]{3,2,1,0:T(2,128)S(1)} %collective-permute-done.1, f32[4,32,32,128]{3,2,1,0:T(8,128)} %param.4, f32[4,32,2,128]{3,2,1,0:T(2,128)S(1)} %collective-permute-done), kind=kLoop, calls=%fused_computation.21 | loop fusion | flops 1179648 | bytes 4718592 | tf_op jit(solution)/shard_map/concatenate | solution.py:20
  16.0 2.3 %fusion.62 = (f32[4,32,36,2]{3,2,1,0:T(8,128)}, f32[4,32,36,2]{3,2,1,0:T(8,128)S(1)}) fusion(f32[4,32,36,128]{3,2,1,0:T(8,128)S(1)} %pad_maximum_fusion.6), kind=kLoop, calls=%fused_computation.114 | loop fusion | bytes 147456 | tf_op jit(solution)/shard_map/slice | solution.py:19
  18.4 2.7 %copy.43 = f32[4,32,36,2]{2,1,3,0:T(8,128)S(1)} copy(f32[4,32,36,2]{3,2,1,0:T(8,128)} %get-tuple-element.7) | data formatting | bytes 73728 | tf_op jit(solution)/shard_map/slice | solution.py:19
  21.1 3.4 %collective-permute-start.2 = (f32[4,32,36,2]{2,1,3,0:T(8,128)S(1)}, f32[4,32,36,2]{2,1,3,0:T(8,128)S(1)}, u32[]{:S(2)}, u32[]{:S(2)}) collective-permute-start(f32[4,32,36,2]{2,1,3,0:T(8,128)S(1)} %copy.43), channel_id=1, source_target_pairs={{0,16},{16,32},{32,48},{1,17},{17,33},{33,49},{2,18},{18,34},{34,5... | collective-permute-start | bytes 110600 | tf_op jit(solution)/shard_map/ppermute | solution.py:22
  24.5 1.0 copy.44
  25.5 2.4 %collective-permute-start.3 = (f32[4,32,36,2]{2,1,3,0:T(8,128)S(1)}, f32[4,32,36,2]{2,1,3,0:T(8,128)S(1)}, u32[]{:S(2)}, u32[]{:S(2)}) collective-permute-start(f32[4,32,36,2]{2,1,3,0:T(8,128)S(1)} %copy.44), channel_id=1, source_target_pairs={{16,0},{32,16},{48,32},{17,1},{33,17},{49,33},{18,2},{34,18},{50,3... | collective-permute-start | bytes 110600 | tf_op jit(solution)/shard_map/ppermute | solution.py:24
  28.0 0.5 compare_and_fusion.1
  28.5 0.0 collective-permute-done.2
  28.5 1.0 copy.45
  29.5 2.9 %collective-permute-done.3 = f32[4,32,36,2]{2,1,3,0:T(8,128)S(1)} collective-permute-done((f32[4,32,36,2]{2,1,3,0:T(8,128)S(1)}, f32[4,32,36,2]{2,1,3,0:T(8,128)S(1)}, u32[]{:S(2)}, u32[]{:S(2)}) %collective-permute-start.3) | collective-permute-done | bytes 36896 | tf_op jit(solution)/shard_map/ppermute | solution.py:24
  32.4 2.5 %copy.46 = f32[4,32,36,2]{3,2,1,0:T(8,128)} copy(f32[4,32,36,2]{2,1,3,0:T(8,128)S(1)} %collective-permute-done.3) | data formatting | bytes 73728 | tf_op jit(solution)/shard_map/ppermute | solution.py:24
  34.9 1.5 %pad_maximum_fusion.11 = (f32[4,2,36,132]{3,2,1,0:T(8,128)S(1)}, f32[4,2,36,132]{3,2,1,0:T(8,128)S(1)}) fusion(f32[4,32,36,2]{3,2,1,0:T(8,128)} %copy.46, f32[4,32,36,2]{3,2,1,0:T(8,128)S(1)} %copy.45, f32[4,32,2,128]{3,2,1,0:T(2,128)S(1)} %collective-permute-done.1, f32[4,32,32,128]{3,2,1,0:T(8,128)} %param.4, f32[4,32,2,128]{3,2,1,0:T(2,128)S(1)} %collective-permute-done), kind=kLoop, calls=%fused_computation.92 | loop fusion | flops 304128 | bytes 2737152 | tf_op jit(solution)/shard_map/slice | solution.py:19
  36.5 2.0 %collective-permute-start.4 = (f32[4,2,36,132]{3,2,1,0:T(8,128)S(1)}, f32[4,2,36,132]{3,2,1,0:T(8,128)}, u32[]{:S(2)}, u32[]{:S(2)}) collective-permute-start(f32[4,2,36,132]{3,2,1,0:T(8,128)S(1)} %get-tuple-element.5), channel_id=1, source_target_pairs={{0,1},{1,2},{2,3},{3,4},{4,5},{5,6},{6,7},{7,8},{8,9},{9,10},{10,1... | collective-permute-start | bytes 456200 | tf_op jit(solution)/shard_map/ppermute | solution.py:22
  38.5 1.5 %collective-permute-start.5 = (f32[4,2,36,132]{3,2,1,0:T(8,128)S(1)}, f32[4,2,36,132]{3,2,1,0:T(8,128)}, u32[]{:S(2)}, u32[]{:S(2)}) collective-permute-start(f32[4,2,36,132]{3,2,1,0:T(8,128)S(1)} %get-tuple-element.6), channel_id=1, source_target_pairs={{1,0},{2,1},{3,2},{4,3},{5,4},{6,5},{7,6},{8,7},{9,8},{10,9},{11,1... | collective-permute-start | bytes 456200 | tf_op jit(solution)/shard_map/ppermute | solution.py:24
  40.0 0.7 broadcast_and_fusion
  40.7 3.3 %copy.59 = f32[32,32,128,4]{2,1,0,3:T(8,128)} copy(f32[32,32,128,4]{2,3,1,0:T(4,128)} %fusion) | data formatting | bytes 4194304 | tf_op jit(solution)/shard_map/cm,mzxy->czxy/dot_general | solution.py:63
  43.9 1.2 dynamic_slice.6
  45.2 1.3 dynamic-slice
  47.1 0.0 collective-permute-done.4
  47.1 0.0 collective-permute-done.5
  47.1 14.4 %fusion.8 = f32[4,34,36,132]{3,2,1,0:T(8,128)S(1)} fusion(f32[4,2,36,132]{3,2,1,0:T(8,128)} %collective-permute-done.5, f32[4,2,36,132]{3,2,1,0:T(8,128)} %collective-permute-done.4, f32[4,32,36,2]{3,2,1,0:T(8,128)} %copy.46, f32[4,32,36,2]{3,2,1,0:T(8,128)S(1)} %copy.45, f32[4,32,2,128]{3,2,1,0:T(2,128)S(1)} %collective-permute-done.1, ...), kind=kLoop, calls=%fused_computation.14 | loop fusion | flops 12925440 | bytes 5322240 | tf_op jit(solution)/shard_map/mul | solution.py:36
  61.5 1.5 %fusion.3 = f32[4,34,34,132]{3,2,1,0:T(8,128)S(1)} fusion(f32[4,34,36,132]{3,2,1,0:T(8,128)S(1)} %fusion.8), kind=kLoop, calls=%fused_computation.7 | loop fusion | flops 2441472 | bytes 9765888 | tf_op jit(solution)/shard_map/mul | solution.py:36
  63.0 3.0 %fusion.1 = f32[4,34,34,130]{3,2,1,0:T(8,128)S(1)} fusion(f32[4,34,34,132]{3,2,1,0:T(8,128)S(1)} %fusion.3), kind=kLoop, calls=%fused_computation.3 | loop fusion | flops 2404480 | bytes 9617920 | tf_op jit(solution)/shard_map/mul | solution.py:36
  66.1 0.2 fusion.16
  66.3 0.1 fusion.17
  66.4 0.2 fusion.18
  66.6 0.2 fusion.27
  66.9 0.8 copy-done.1
  67.7 1.1 fusion.26
  68.8 0.5 fusion.34
  69.2 0.0 copy-start.2
  69.2 0.3 fusion.21
  69.5 0.2 fusion.19
  69.7 0.1 fusion.28
  69.8 26.1 %all-gather = f32[512,128]{1,0:T(8,128)S(1)} all-gather(f32[32,128]{1,0:T(8,128)S(1)} %fusion.34), channel_id=2, replica_groups=mesh['gx'=8,'gy'=4,'gz'=16] {'gz'}, dimensions={0}, use_global_device_ids=true | all-gather | bytes 278528 | tf_op jit(solution)/shard_map/all_gather | solution.py:94
  96.0 1.0 fusion.50
  97.0 0.7 multiply_add_fusion
  97.7 0.8 multiply_reduce_fusion
  98.6 46.0 %all-reduce = f32[3,32,128]{2,1,0:T(8,128)S(1)} all-reduce(f32[3,32,128]{2,1,0:T(8,128)S(1)} %copy.48), channel_id=3, replica_groups=mesh['gx'=8,'gy'=4,'gz'=16] {'gz'}, use_global_device_ids=true, to_apply=%region_3.4.clone | all-reduce | flops 12288 | bytes 98304
  144.7 0.6 pad_maximum_fusion.12
  (9 shorter events, 0.1 us)
Async XLA Ops:
  0.0 8.0 %copy-start = (f32[4,16]{1,0:T(4,128)S(1)}, f32[4,16]{1,0:T(4,128)}, u32[]{:S(2)}) copy-start(f32[4,16]{1,0:T(4,128)} %param.7) | copy-start | bytes 772
  1.3 11.1 %collective-permute-start = (f32[4,32,2,128]{3,2,1,0:T(2,128)S(1)}, f32[4,32,2,128]{3,2,1,0:T(2,128)S(1)}, u32[]{:S(2)}, u32[]{:S(2)}) collective-permute-start(f32[4,32,2,128]{3,2,1,0:T(2,128)S(1)} %get-tuple-element.9), channel_id=1, source_target_pairs={{0,64},{64,128},{128,192},{192,256},{256,320},{320,384},{384,448},... | collective-permute-start | bytes 393224 | tf_op jit(solution)/shard_map/ppermute | solution.py:22
  6.0 8.1 %collective-permute-start.1 = (f32[4,32,2,128]{3,2,1,0:T(2,128)S(1)}, f32[4,32,2,128]{3,2,1,0:T(2,128)S(1)}, u32[]{:S(2)}, u32[]{:S(2)}) collective-permute-start(f32[4,32,2,128]{3,2,1,0:T(2,128)S(1)} %get-tuple-element.10), channel_id=1, source_target_pairs={{64,0},{128,64},{192,128},{256,192},{320,256},{384,320},{448,384},... | collective-permute-start | bytes 393224 | tf_op jit(solution)/shard_map/ppermute | solution.py:24
  21.1 7.4 %collective-permute-start.2 = (f32[4,32,36,2]{2,1,3,0:T(8,128)S(1)}, f32[4,32,36,2]{2,1,3,0:T(8,128)S(1)}, u32[]{:S(2)}, u32[]{:S(2)}) collective-permute-start(f32[4,32,36,2]{2,1,3,0:T(8,128)S(1)} %copy.43), channel_id=1, source_target_pairs={{0,16},{16,32},{32,48},{1,17},{17,33},{33,49},{2,18},{18,34},{34,5... | collective-permute-start | bytes 110600 | tf_op jit(solution)/shard_map/ppermute | solution.py:22
  25.5 6.9 %collective-permute-start.3 = (f32[4,32,36,2]{2,1,3,0:T(8,128)S(1)}, f32[4,32,36,2]{2,1,3,0:T(8,128)S(1)}, u32[]{:S(2)}, u32[]{:S(2)}) collective-permute-start(f32[4,32,36,2]{2,1,3,0:T(8,128)S(1)} %copy.44), channel_id=1, source_target_pairs={{16,0},{32,16},{48,32},{17,1},{33,17},{49,33},{18,2},{34,18},{50,3... | collective-permute-start | bytes 110600 | tf_op jit(solution)/shard_map/ppermute | solution.py:24
  36.5 10.6 %collective-permute-start.4 = (f32[4,2,36,132]{3,2,1,0:T(8,128)S(1)}, f32[4,2,36,132]{3,2,1,0:T(8,128)}, u32[]{:S(2)}, u32[]{:S(2)}) collective-permute-start(f32[4,2,36,132]{3,2,1,0:T(8,128)S(1)} %get-tuple-element.5), channel_id=1, source_target_pairs={{0,1},{1,2},{2,3},{3,4},{4,5},{5,6},{6,7},{7,8},{8,9},{9,10},{10,1... | collective-permute-start | bytes 456200 | tf_op jit(solution)/shard_map/ppermute | solution.py:22
  38.5 8.6 %collective-permute-start.5 = (f32[4,2,36,132]{3,2,1,0:T(8,128)S(1)}, f32[4,2,36,132]{3,2,1,0:T(8,128)}, u32[]{:S(2)}, u32[]{:S(2)}) collective-permute-start(f32[4,2,36,132]{3,2,1,0:T(8,128)S(1)} %get-tuple-element.6), channel_id=1, source_target_pairs={{1,0},{2,1},{3,2},{4,3},{5,4},{6,5},{7,6},{8,7},{9,8},{10,9},{11,1... | collective-permute-start | bytes 456200 | tf_op jit(solution)/shard_map/ppermute | solution.py:24
  66.1 1.6 %copy-start.1 = (f32[32,32,128,4]{2,1,0,3:T(8,128)S(1)}, f32[32,32,128,4]{2,1,0,3:T(8,128)}, u32[]{:S(2)}) copy-start(f32[32,32,128,4]{2,1,0,3:T(8,128)} %copy.59) | copy-start | bytes 6291460
  69.2 26.7 %copy-start.2 = (s32[16]{0:T(128)S(1)}, s32[16]{0:T(128)}, u32[]{:S(2)}) copy-start(s32[16]{0:T(128)} %param.6) | copy-start | bytes 196
where the time goes:
time: 146 us; the launch traced here: 145 us
  blocking collectives  72.1 us (49%)
  other arithmetic  28.8 us (20%)
  local copies, waits for them, and re-layouts  17.6 us (12%)
  starting transfers between devices  15.9 us (11%)
  matrix products  5.49 us (4%)
  waiting for transfers between devices  4.51 us (3%)
    unnamed x1, blocking collectives  46 us
    all_gather x1, blocking collectives, on_device(): depths = lax.all_gather(depth[None], 'gz', axis=0, tiled=True)  26.1 us
    mul x6, other arithmetic, blur_axis(): return (lower + 2.0 * middle + upper) * 0.25  19.5 us
    ppermute x3, starting transfers between devices, extended(): lax.ppermute(tail, axis, [(i, (i + 1) % count) for i in range(ends)])  10.1 us
    slice x3, local copies, waits for them, and re-layouts, extended(): lax.slice_in_dim(cells, cells.shape[dim] - width, cells.shape[dim], axis=...  6.39 us
    ppermute x3, starting transfers between devices, extended(): lax.ppermute(head, axis, [((i + 1) % count, i) for i in range(ends)])  5.83 us
    ppermute x3, waiting for transfers between devices, extended(): lax.ppermute(head, axis, [((i + 1) % count, i) for i in range(ends)])  4.5 us
    dot_general x1, matrix products, shade_brick(): jnp.einsum('cm,mzxy->czxy', table, onehot, precision=lax.Precision.HIGHEST)  4.49 us
  transfers between devices with their start and end apart: 6, of which 2 were waited for; matrix products, arithmetic and copies ran while one was open for 9% of the time, Pallas kernels for 0%

commit v1 on v0

--- a/solution.py
+++ b/solution.py
@@ -91,7 +91,9 @@
     colour, depth = shade_brick(inner, density, material, table, depth_total)
     rows = xsize // layers
     layer_index = lax.axis_index("gz")
-    depths = lax.all_gather(depth[None], "gz", axis=0, tiled=True)
+    depths = jnp.concatenate(
+        lax.all_to_all(jnp.stack([depth[None]] * lax.axis_size("gz")), "gz", 0, 0), axis=0
+    )
     own_rank = depth_order[layer_index]
     nearer = (depth_order < own_rank).astype(jnp.float32)
     atten = jnp.einsum("g,gxy->xy", nearer, depths, precision=lax.Precision.HIGHEST)

time: 146 us -> 147 us (level)
  the two profiles are of different devices: /device:TPU:26 before, /device:TPU:24 now
where the time goes in v1:
time: 147 us; the launch traced here: 146 us
  blocking collectives  48.1 us (33%)
  other arithmetic  38.9 us (26%)
  starting transfers between devices  28.7 us (20%)
  local copies, waits for them, and re-layouts  17.9 us (12%)
  waiting for transfers between devices  6.18 us (4%)
  matrix products  5.5 us (4%)
    unnamed x1, blocking collectives  48.1 us
    mul x6, other arithmetic, blur_axis(): return (lower + 2.0 * middle + upper) * 0.25  21.6 us
    all_to_all x1, starting transfers between devices, on_device(): lax.all_to_all(jnp.stack([depth[None]] * lax.axis_size('gz')), 'gz', 0, 0)  13.9 us
    ppermute x3, starting transfers between devices, extended(): lax.ppermute(tail, axis, [(i, (i + 1) % count) for i in range(ends)])  10.1 us
    slice x3, local copies, waits for them, and re-layouts, extended(): lax.slice_in_dim(cells, cells.shape[dim] - width, cells.shape[dim], axis=...  6.4 us
    ppermute x3, waiting for transfers between devices, extended(): lax.ppermute(head, axis, [((i + 1) % count, i) for i in range(ends)])  5.65 us
    ppermute x3, starting transfers between devices, extended(): lax.ppermute(head, axis, [((i + 1) % count, i) for i in range(ends)])  4.67 us
    dot_general x1, matrix products, shade_brick(): jnp.einsum('cm,mzxy->czxy', table, onehot, precision=lax.Precision.HIGHEST)  4.5 us
  transfers between devices with their start and end apart: 7, of which 3 were waited for; matrix products, arithmetic and copies ran while one was open for 17% of the time, Pallas kernels for 0%

profile of v1, /device:TPU:24, one launch (start us, length us, event | category | flops | bytes accessed | tf_op | source)
XLA Modules:
  0.0 146.0 jit_solution(13071434346959034304)
XLA Ops:
  0.0 1.3 fusion.63
  1.3 4.7 %collective-permute-start = (f32[4,32,2,128]{3,2,1,0:T(2,128)S(1)}, f32[4,32,2,128]{3,2,1,0:T(2,128)S(1)}, u32[]{:S(2)}, u32[]{:S(2)}) collective-permute-start(f32[4,32,2,128]{3,2,1,0:T(2,128)S(1)} %get-tuple-element.9), channel_id=1, source_target_pairs={{0,64},{64,128},{128,192},{192,256},{256,320},{320,384},{384,448},... | collective-permute-start | bytes 393224 | tf_op jit(solution)/shard_map/ppermute | solution.py:22
  6.0 1.9 %collective-permute-start.1 = (f32[4,32,2,128]{3,2,1,0:T(2,128)S(1)}, f32[4,32,2,128]{3,2,1,0:T(2,128)S(1)}, u32[]{:S(2)}, u32[]{:S(2)}) collective-permute-start(f32[4,32,2,128]{3,2,1,0:T(2,128)S(1)} %get-tuple-element.10), channel_id=1, source_target_pairs={{64,0},{128,64},{192,128},{256,192},{320,256},{384,320},{448,384},... | collective-permute-start | bytes 393224 | tf_op jit(solution)/shard_map/ppermute | solution.py:24
  8.0 4.5 %fusion = f32[32,32,128,4]{2,3,1,0:T(4,128)} fusion(s32[32,32,128]{2,1,0:T(8,128)} %param.5, f32[4,16]{1,0:T(4,128)S(1)} %copy-done), kind=kOutput, calls=%fused_computation.1 | convolution fusion | flops 102760448 | bytes 2621696 | tf_op jit(solution)/shard_map/cm,mzxy->czxy/dot_general | solution.py:63
  12.5 0.0 collective-permute-done
  12.5 1.6 %collective-permute-done.1 = f32[4,32,2,128]{3,2,1,0:T(2,128)S(1)} collective-permute-done((f32[4,32,2,128]{3,2,1,0:T(2,128)S(1)}, f32[4,32,2,128]{3,2,1,0:T(2,128)S(1)}, u32[]{:S(2)}, u32[]{:S(2)}) %collective-permute-start.1) | collective-permute-done | bytes 131104 | tf_op jit(solution)/shard_map/ppermute | solution.py:24
  14.1 1.9 %pad_maximum_fusion.6 = f32[4,32,36,128]{3,2,1,0:T(8,128)S(1)} fusion(f32[4,32,2,128]{3,2,1,0:T(2,128)S(1)} %collective-permute-done.1, f32[4,32,32,128]{3,2,1,0:T(8,128)} %param.4, f32[4,32,2,128]{3,2,1,0:T(2,128)S(1)} %collective-permute-done), kind=kLoop, calls=%fused_computation.21 | loop fusion | flops 1179648 | bytes 4718592 | tf_op jit(solution)/shard_map/concatenate | solution.py:20
  16.0 2.4 %fusion.62 = (f32[4,32,36,2]{3,2,1,0:T(8,128)}, f32[4,32,36,2]{3,2,1,0:T(8,128)S(1)}) fusion(f32[4,32,36,128]{3,2,1,0:T(8,128)S(1)} %pad_maximum_fusion.6), kind=kLoop, calls=%fused_computation.114 | loop fusion | bytes 147456 | tf_op jit(solution)/shard_map/slice | solution.py:19
  18.4 2.7 %copy.43 = f32[4,32,36,2]{2,1,3,0:T(8,128)S(1)} copy(f32[4,32,36,2]{3,2,1,0:T(8,128)} %get-tuple-element.7) | data formatting | bytes 73728 | tf_op jit(solution)/shard_map/slice | solution.py:19
  21.1 3.4 %collective-permute-start.2 = (f32[4,32,36,2]{2,1,3,0:T(8,128)S(1)}, f32[4,32,36,2]{2,1,3,0:T(8,128)S(1)}, u32[]{:S(2)}, u32[]{:S(2)}) collective-permute-start(f32[4,32,36,2]{2,1,3,0:T(8,128)S(1)} %copy.43), channel_id=1, source_target_pairs={{0,16},{16,32},{32,48},{1,17},{17,33},{33,49},{2,18},{18,34},{34,5... | collective-permute-start | bytes 110600 | tf_op jit(solution)/shard_map/ppermute | solution.py:22
  24.5 1.0 copy.44
  25.6 1.3 collective-permute-start.3
  26.9 0.5 compare_and_fusion.1
  27.4 0.0 collective-permute-done.2
  27.4 1.0 copy.45
  28.4 4.0 %collective-permute-done.3 = f32[4,32,36,2]{2,1,3,0:T(8,128)S(1)} collective-permute-done((f32[4,32,36,2]{2,1,3,0:T(8,128)S(1)}, f32[4,32,36,2]{2,1,3,0:T(8,128)S(1)}, u32[]{:S(2)}, u32[]{:S(2)}) %collective-permute-start.3) | collective-permute-done | bytes 36896 | tf_op jit(solution)/shard_map/ppermute | solution.py:24
  32.4 2.5 %copy.46 = f32[4,32,36,2]{3,2,1,0:T(8,128)} copy(f32[4,32,36,2]{2,1,3,0:T(8,128)S(1)} %collective-permute-done.3) | data formatting | bytes 73728 | tf_op jit(solution)/shard_map/ppermute | solution.py:24
  35.0 1.5 %pad_maximum_fusion.11 = (f32[4,2,36,132]{3,2,1,0:T(8,128)S(1)}, f32[4,2,36,132]{3,2,1,0:T(8,128)S(1)}) fusion(f32[4,32,36,2]{3,2,1,0:T(8,128)} %copy.46, f32[4,32,36,2]{3,2,1,0:T(8,128)S(1)} %copy.45, f32[4,32,2,128]{3,2,1,0:T(2,128)S(1)} %collective-permute-done.1, f32[4,32,32,128]{3,2,1,0:T(8,128)} %param.4, f32[4,32,2,128]{3,2,1,0:T(2,128)S(1)} %collective-permute-done), kind=kLoop, calls=%fused_computation.92 | loop fusion | flops 304128 | bytes 2737152 | tf_op jit(solution)/shard_map/slice | solution.py:19
  36.5 2.0 %collective-permute-start.4 = (f32[4,2,36,132]{3,2,1,0:T(8,128)S(1)}, f32[4,2,36,132]{3,2,1,0:T(8,128)}, u32[]{:S(2)}, u32[]{:S(2)}) collective-permute-start(f32[4,2,36,132]{3,2,1,0:T(8,128)S(1)} %get-tuple-element.5), channel_id=1, source_target_pairs={{0,1},{1,2},{2,3},{3,4},{4,5},{5,6},{6,7},{7,8},{8,9},{9,10},{10,1... | collective-permute-start | bytes 456200 | tf_op jit(solution)/shard_map/ppermute | solution.py:22
  38.5 1.5 %collective-permute-start.5 = (f32[4,2,36,132]{3,2,1,0:T(8,128)S(1)}, f32[4,2,36,132]{3,2,1,0:T(8,128)}, u32[]{:S(2)}, u32[]{:S(2)}) collective-permute-start(f32[4,2,36,132]{3,2,1,0:T(8,128)S(1)} %get-tuple-element.6), channel_id=1, source_target_pairs={{1,0},{2,1},{3,2},{4,3},{5,4},{6,5},{7,6},{8,7},{9,8},{10,9},{11,1... | collective-permute-start | bytes 456200 | tf_op jit(solution)/shard_map/ppermute | solution.py:24
  40.0 0.7 broadcast_and_fusion
  40.7 3.2 %copy.59 = f32[32,32,128,4]{2,1,0,3:T(8,128)} copy(f32[32,32,128,4]{2,3,1,0:T(4,128)} %fusion) | data formatting | bytes 4194304 | tf_op jit(solution)/shard_map/cm,mzxy->czxy/dot_general | solution.py:63
  43.9 1.2 dynamic_slice.6
  45.2 1.3 dynamic-slice
  47.0 0.0 collective-permute-done.4
  47.0 0.0 collective-permute-done.5
  47.0 14.4 %fusion.8 = f32[4,34,36,132]{3,2,1,0:T(8,128)S(1)} fusion(f32[4,2,36,132]{3,2,1,0:T(8,128)} %collective-permute-done.5, f32[4,2,36,132]{3,2,1,0:T(8,128)} %collective-permute-done.4, f32[4,32,36,2]{3,2,1,0:T(8,128)} %copy.46, f32[4,32,36,2]{3,2,1,0:T(8,128)S(1)} %copy.45, f32[4,32,2,128]{3,2,1,0:T(2,128)S(1)} %collective-permute-done.1, ...), kind=kLoop, calls=%fused_computation.14 | loop fusion | flops 12925440 | bytes 5322240 | tf_op jit(solution)/shard_map/mul | solution.py:36
  61.5 1.5 %fusion.3 = f32[4,34,34,132]{3,2,1,0:T(8,128)S(1)} fusion(f32[4,34,36,132]{3,2,1,0:T(8,128)S(1)} %fusion.8), kind=kLoop, calls=%fused_computation.7 | loop fusion | flops 2441472 | bytes 9765888 | tf_op jit(solution)/shard_map/mul | solution.py:36
  63.0 3.0 %fusion.1 = f32[4,34,34,130]{3,2,1,0:T(8,128)S(1)} fusion(f32[4,34,34,132]{3,2,1,0:T(8,128)S(1)} %fusion.3), kind=kLoop, calls=%fused_computation.3 | loop fusion | flops 2404480 | bytes 9617920 | tf_op jit(solution)/shard_map/mul | solution.py:36
  66.1 0.2 fusion.16
  66.3 0.1 fusion.17
  66.4 0.2 fusion.18
  66.6 0.2 fusion.27
  66.8 1.3 fusion.21
  68.2 1.2 fusion.19
  69.4 0.1 fusion.28
  69.5 0.4 copy-done.2
  69.9 0.5 fusion.34
  70.4 0.7 stack.3
  71.1 13.9 %all-to-all-start = ((f32[16,1,32,128]{3,2,1,0:T(8,128)}), f32[16,1,32,128]{3,2,1,0:T(8,128)S(1)}, u32[]{:S(2)}, u32[]{:S(2)}) async-start(f32[16,1,32,128]{3,2,1,0:T(8,128)} %stack.3), calls=%async_computation | async-start | bytes 524288 | tf_op jit(solution)/shard_map/all_to_all | solution.py:95
  85.0 0.0 copy-start.3
  85.0 3.4 %multiply_add_fusion = f32[32,32,128]{2,1,0:T(8,128)S(1)} fusion(f32[32,34,128]{2,1,0:T(8,128)S(1)} %fusion.28, f32[32,32,130]{2,1,0:T(8,128)} %fusion.19, f32[32,32,130]{2,1,0:T(8,128)} %fusion.21), kind=kLoop, calls=%fused_computation.80 | loop fusion | flops 3538944 | bytes 5242880 | tf_op jit(solution)/shard_map/add | solution.py:58
  88.5 4.2 %fusion.26 = f32[32,32,128]{2,1,0:T(8,128)S(1)} fusion(f32[4,32,32,128]{3,2,1,0:T(8,128)S(1)} %bitcast.45, f32[4,34,34,130]{3,2,1,0:T(8,128)} %copy-done.1), kind=kOutput, calls=%fused_computation.52 | output fusion | flops 5898240 | bytes 1572864 | tf_op jit(solution)/shard_map/jit(cumsum)/reduce_window_sum | solution.py:66
  92.7 3.0 %multiply_reduce_fusion = f32[3,32,128]{2,1,0:T(8,128)S(1)} fusion(f32[4,34,34,130]{3,2,1,0:T(8,128)} %copy-done.1, f32[4,32,32,128]{3,2,1,0:T(8,128)S(1)} %bitcast.46, f32[32,32,128]{2,1,0:T(8,128)S(1)} %multiply_add_fusion, f32[32,32,128]{2,1,0:T(8,128)S(1)} %fusion.26), kind=kLoop, calls=%fused_computation.31 | loop fusion | flops 3526656 | bytes 4243456 | tf_op jit(solution)/shard_map/reduce_sum | solution.py:68
  95.7 0.5 all-to-all-done
  96.2 1.0 fusion.50
  97.3 48.1 %all-reduce = f32[3,32,128]{2,1,0:T(8,128)S(1)} all-reduce(f32[3,32,128]{2,1,0:T(8,128)S(1)} %copy.48), channel_id=2, replica_groups=mesh['gx'=8,'gy'=4,'gz'=16] {'gz'}, use_global_device_ids=true, to_apply=%region_3.4.clone | all-reduce | flops 12288 | bytes 98304
  145.4 0.6 pad_maximum_fusion.12
  (13 shorter events, 0.1 us)
Async XLA Ops:
  0.0 8.0 %copy-start = (f32[4,16]{1,0:T(4,128)S(1)}, f32[4,16]{1,0:T(4,128)}, u32[]{:S(2)}) copy-start(f32[4,16]{1,0:T(4,128)} %param.7) | copy-start | bytes 772
  1.3 11.1 %collective-permute-start = (f32[4,32,2,128]{3,2,1,0:T(2,128)S(1)}, f32[4,32,2,128]{3,2,1,0:T(2,128)S(1)}, u32[]{:S(2)}, u32[]{:S(2)}) collective-permute-start(f32[4,32,2,128]{3,2,1,0:T(2,128)S(1)} %get-tuple-element.9), channel_id=1, source_target_pairs={{0,64},{64,128},{128,192},{192,256},{256,320},{320,384},{384,448},... | collective-permute-start | bytes 393224 | tf_op jit(solution)/shard_map/ppermute | solution.py:22
  6.0 8.1 %collective-permute-start.1 = (f32[4,32,2,128]{3,2,1,0:T(2,128)S(1)}, f32[4,32,2,128]{3,2,1,0:T(2,128)S(1)}, u32[]{:S(2)}, u32[]{:S(2)}) collective-permute-start(f32[4,32,2,128]{3,2,1,0:T(2,128)S(1)} %get-tuple-element.10), channel_id=1, source_target_pairs={{64,0},{128,64},{192,128},{256,192},{320,256},{384,320},{448,384},... | collective-permute-start | bytes 393224 | tf_op jit(solution)/shard_map/ppermute | solution.py:24
  21.1 6.2 %collective-permute-start.2 = (f32[4,32,36,2]{2,1,3,0:T(8,128)S(1)}, f32[4,32,36,2]{2,1,3,0:T(8,128)S(1)}, u32[]{:S(2)}, u32[]{:S(2)}) collective-permute-start(f32[4,32,36,2]{2,1,3,0:T(8,128)S(1)} %copy.43), channel_id=1, source_target_pairs={{0,16},{16,32},{32,48},{1,17},{17,33},{33,49},{2,18},{18,34},{34,5... | collective-permute-start | bytes 110600 | tf_op jit(solution)/shard_map/ppermute | solution.py:22
  25.6 6.9 %collective-permute-start.3 = (f32[4,32,36,2]{2,1,3,0:T(8,128)S(1)}, f32[4,32,36,2]{2,1,3,0:T(8,128)S(1)}, u32[]{:S(2)}, u32[]{:S(2)}) collective-permute-start(f32[4,32,36,2]{2,1,3,0:T(8,128)S(1)} %copy.44), channel_id=1, source_target_pairs={{16,0},{32,16},{48,32},{17,1},{33,17},{49,33},{18,2},{34,18},{50,3... | collective-permute-start | bytes 110600 | tf_op jit(solution)/shard_map/ppermute | solution.py:24
  36.5 10.6 %collective-permute-start.4 = (f32[4,2,36,132]{3,2,1,0:T(8,128)S(1)}, f32[4,2,36,132]{3,2,1,0:T(8,128)}, u32[]{:S(2)}, u32[]{:S(2)}) collective-permute-start(f32[4,2,36,132]{3,2,1,0:T(8,128)S(1)} %get-tuple-element.5), channel_id=1, source_target_pairs={{0,1},{1,2},{2,3},{3,4},{4,5},{5,6},{6,7},{7,8},{8,9},{9,10},{10,1... | collective-permute-start | bytes 456200 | tf_op jit(solution)/shard_map/ppermute | solution.py:22
  38.5 8.6 %collective-permute-start.5 = (f32[4,2,36,132]{3,2,1,0:T(8,128)S(1)}, f32[4,2,36,132]{3,2,1,0:T(8,128)}, u32[]{:S(2)}, u32[]{:S(2)}) collective-permute-start(f32[4,2,36,132]{3,2,1,0:T(8,128)S(1)} %get-tuple-element.6), channel_id=1, source_target_pairs={{1,0},{2,1},{3,2},{4,3},{5,4},{6,5},{7,6},{8,7},{9,8},{10,9},{11,1... | collective-permute-start | bytes 456200 | tf_op jit(solution)/shard_map/ppermute | solution.py:24
  66.0 3.5 %copy-start.1 = (f32[4,34,34,130]{3,2,1,0:T(8,128)}, f32[4,34,34,130]{3,2,1,0:T(8,128)S(1)}, u32[]{:S(2)}) copy-start(f32[4,34,34,130]{3,2,1,0:T(8,128)S(1)} %fusion.1) | copy-start | bytes 7213444
  66.8 3.1 %copy-start.2 = (f32[32,32,128,4]{2,1,0,3:T(8,128)S(1)}, f32[32,32,128,4]{2,1,0,3:T(8,128)}, u32[]{:S(2)}) copy-start(f32[32,32,128,4]{2,1,0,3:T(8,128)} %copy.59) | copy-start | bytes 6291460
  71.1 25.1 %all-to-all-start = ((f32[16,1,32,128]{3,2,1,0:T(8,128)}), f32[16,1,32,128]{3,2,1,0:T(8,128)S(1)}, u32[]{:S(2)}, u32[]{:S(2)}) async-start(f32[16,1,32,128]{3,2,1,0:T(8,128)} %stack.3), calls=%async_computation | async-start | bytes 524288 | tf_op jit(solution)/shard_map/all_to_all | solution.py:95
  85.0 11.2 %copy-start.3 = (s32[16]{0:T(128)S(1)}, s32[16]{0:T(128)}, u32[]{:S(2)}) copy-start(s32[16]{0:T(128)} %param.6) | copy-start | bytes 196
